TPU v7x, 128 devices: a whole 4x4x4 slice. The times are simulated.
128 devices in a mesh: seq: 128 (over x, y, z, core).
Axes of the slice: x: 4, y: 4, z: 4, core: 2. Of those that a mesh axis runs over, the one named last changes fastest.
Arguments:
- inputs: bfloat16 [2, 32768, 1536], P(None, 'seq'), may hold values from -8 to 8
- ln_gain: float32 [1536], replicated, may hold values from 0.25 to 1.75
- w_in: bfloat16 [1536, 3072], replicated, may hold values from -0.15625 to 0.15625
- kernel: float32 [32, 1536], replicated, may hold values from -1 to 1
- bn_gain: float32 [1536], replicated, may hold values from 0.25 to 1.75
- bn_bias: float32 [1536], replicated, may hold values from -0.6 to 0.6
- w_out: bfloat16 [1536, 1536], replicated, may hold values from -0.15625 to 0.15625
- cotangent: bfloat16 [2, 32768, 1536], P(None, 'seq'), may hold values from -24 to 24
Outputs:
- outputs: bfloat16 [2, 32768, 1536], P(None, 'seq')
- d_inputs: bfloat16 [2, 32768, 1536], P(None, 'seq')
- d_w_out: float32 [1536, 1536], P('seq')
- d_kernel: float32 [32, 1536], replicated
- d_bn_gain: float32 [1536], replicated
- d_bn_bias: float32 [1536], replicated
All inputs are finite; a program needn't handle non-finite values.
Results may differ from a plain program's by a relative error of at most 0.0075.
Values may be sent and summed in bfloat16 or wider, within the bound.
A program may use at most 128 MiB of HBM per device.

v0:
```python
import jax
import jax.numpy as jnp
from jax import lax
from jax.sharding import PartitionSpec as P

D = 1536
K = 32
FRAMES_DEV = 256
UTT = 2
EPSILON = 1e-05


def with_halo(block, sides, width):
    for axis, dim in sides:
        count = lax.axis_size(axis)
        forward = [(i, i + 1) for i in range(count - 1)]
        backward = [(target, source) for source, target in forward]
        low = lax.ppermute(
            lax.slice_in_dim(block, block.shape[dim] - width, None, axis=dim), axis, forward
        )
        high = lax.ppermute(lax.slice_in_dim(block, 0, width, axis=dim), axis, backward)
        block = jnp.concatenate([low, block, high], axis=dim)
    return block


def on_device(inputs, ln_gain, w_in, kernel, bn_gain, bn_bias, w_out, cotangent):
    devices_seq = lax.axis_size("seq")
    frame_total = UTT * FRAMES_DEV * devices_seq
    rows_here = UTT * FRAMES_DEV
    x_float = inputs.astype(jnp.float32)
    ln_mean = jnp.mean(x_float, axis=-1, keepdims=True)
    centred = x_float - ln_mean
    ln_rstd = lax.rsqrt(jnp.mean(centred * centred, axis=-1, keepdims=True) + EPSILON)
    ln_hat = centred * ln_rstd
    normed = (ln_hat * ln_gain).astype(jnp.bfloat16).reshape(rows_here, D)
    proj = jnp.dot(normed, w_in, preferred_element_type=jnp.float32)
    value_half = proj[:, :D]
    gate_sig = jax.nn.sigmoid(proj[:, D:])
    gated = (value_half * gate_sig).astype(jnp.bfloat16).reshape(UTT, FRAMES_DEV, D)
    padded = with_halo(gated, (("seq", 1),), 16)
    conv_out = jnp.zeros((UTT, FRAMES_DEV, D), jnp.float32)
    for tap_index in range(K):
        conv_out = conv_out + kernel[tap_index] * padded[
            :, tap_index + 1 : tap_index + 1 + FRAMES_DEV
        ].astype(jnp.float32)
    bn_mean = lax.psum(jnp.sum(conv_out, axis=(0, 1)), "seq") / frame_total
    deviate = conv_out - bn_mean
    bn_var = lax.psum(jnp.sum(deviate * deviate, axis=(0, 1)), "seq") / frame_total
    bn_rstd = lax.rsqrt(bn_var + EPSILON)
    normed_bn = deviate * bn_rstd
    bn_out = normed_bn * bn_gain + bn_bias
    act_sig = jax.nn.sigmoid(bn_out)
    act = (bn_out * act_sig).astype(jnp.bfloat16).reshape(rows_here, D)
    branch = lax.dot_general(
        act, w_out, (((1,), (1,)), ((), ())), preferred_element_type=jnp.float32
    )
    outputs = (
        (x_float.reshape(rows_here, D) + branch).astype(jnp.bfloat16).reshape(UTT, FRAMES_DEV, D)
    )
    cot_rows = cotangent.reshape(rows_here, D)
    d_w_out = lax.psum_scatter(
        lax.dot_general(
            cot_rows, act, (((0,), (0,)), ((), ())), preferred_element_type=jnp.float32
        ),
        "seq",
        scatter_dimension=0,
        tiled=True,
    )
    d_act = jnp.dot(cot_rows, w_out, preferred_element_type=jnp.float32)
    d_bn = d_act.reshape(UTT, FRAMES_DEV, D) * (act_sig + bn_out * act_sig * (1.0 - act_sig))
    scaled_grad = d_bn * bn_gain
    local_bias = jnp.sum(d_bn, axis=(0, 1))
    local_gain = jnp.sum(d_bn * normed_bn, axis=(0, 1))
    d_bn_bias, d_bn_gain = lax.psum((local_bias, local_gain), "seq")
    mean_grad = bn_gain * d_bn_bias / frame_total
    mean_cross = bn_gain * d_bn_gain / frame_total
    d_conv = bn_rstd * (scaled_grad - mean_grad - normed_bn * mean_cross)
    kernel_rows = []
    for tap_index in range(K):
        window = padded[:, tap_index + 1 : tap_index + 1 + FRAMES_DEV].astype(jnp.float32)
        kernel_rows.append(jnp.sum(window * d_conv, axis=(0, 1)))
    d_kernel = lax.psum(jnp.stack(kernel_rows), "seq")
    grad_padded = with_halo(d_conv.astype(jnp.bfloat16), (("seq", 1),), 16).astype(d_conv.dtype)
    d_gated = jnp.zeros((UTT, FRAMES_DEV, D), jnp.float32)
    for tap_index in range(K):
        d_gated = (
            d_gated
            + kernel[tap_index] * grad_padded[:, 31 - tap_index : 31 - tap_index + FRAMES_DEV]
        )
    d_gated = d_gated.reshape(rows_here, D)
    d_value = d_gated * gate_sig
    d_gate = d_gated * value_half * gate_sig * (1.0 - gate_sig)
    d_proj = jnp.concatenate([d_value, d_gate], axis=-1).astype(jnp.bfloat16)
    d_normed = lax.dot_general(
        d_proj, w_in, (((1,), (1,)), ((), ())), preferred_element_type=jnp.float32
    )
    d_hat = d_normed.reshape(UTT, FRAMES_DEV, D) * ln_gain
    d_layer = ln_rstd * (
        d_hat
        - jnp.mean(d_hat, axis=-1, keepdims=True)
        - ln_hat * jnp.mean(d_hat * ln_hat, axis=-1, keepdims=True)
    )
    d_inputs = (cotangent.astype(jnp.float32) + d_layer).astype(jnp.bfloat16)
    return (outputs, d_inputs, d_w_out, d_kernel, d_bn_gain, d_bn_bias)


def solution(mesh):
    return jax.shard_map(
        on_device,
        mesh=mesh,
        in_specs=(P(None, "seq", None), P(), P(), P(), P(), P(), P(), P(None, "seq", None)),
        out_specs=(P(None, "seq", None), P(None, "seq", None), P("seq", None), P(), P(), P()),
        check_vma=False,
    )
```

profile of v0, /device:TPU:1, one launch (start us, length us, event | category | flops | bytes accessed | tf_op | source)
XLA Modules:
  0.0 475.8 jit_solution(6670448868981798242)
XLA Ops:
  7.2 0.0 copy-start.1
  7.2 0.0 copy-start.51
  7.2 0.0 all-reduce.5.cloned.1.call-start
  7.2 1.8 convert_reduce_fusion
  9.1 2.0 multiply_reduce_fusion.4
  11.0 0.5 multiply_convert_fusion.1
  11.6 0.0 copy-done.55
  11.6 7.6 %fusion.148 = f32[512,3072]{1,0:T(8,128)S(1)} fusion(bf16[512,1536]{1,0:T(8,128)(2,1)S(1)} %bitcast.51, bf16[1536,3072]{1,0:T(8,128)(2,1)} %param.10), kind=kOutput, calls=%fused_computation.333 | convolution fusion | flops 4831838208 | bytes 17301504 | tf_op jit(solution)/shard_map/dot_general | solution.py:36
  19.2 0.8 multiply_convert_fusion
  20.1 1.7 copy-done
  21.8 0.7 fusion.147
  22.5 3.3 collective-permute-start.1
  25.8 3.6 collective-permute-start
  29.3 0.9 slice_reduce_fusion.31
  30.3 0.2 slice_reduce_fusion.30
  30.6 0.7 collective-permute-done
  31.3 17.2 %fusion.144 = (f32[1536]{0:T(1024)S(1)}, f32[2,256,1536]{2,1,0:T(8,128)}) fusion(bf16[2,16,1536]{2,1,0:T(8,128)(2,1)S(1)} %collective-permute-done.1, bf16[2,256,1536]{2,1,0:T(8,128)(2,1)S(1)} %bitcast.42, f32[1536]{0:T(1024)S(1)} %get-tuple-element.82, f32[1536]{0:T(1024)S(1)} %get-tuple-element.83, f32[1536]{0:T(1024)S(1)} %get-tuple-element.53, ...), kind=kLoop, calls=%fused_computation.330 | loop fusion | flops 148634112 | bytes 5117952 | tf_op jit(solution)/shard_map/reduce_sum | solution.py:46
  48.5 73.1 %psum.35 = f32[1536]{0:T(1024)S(1)} all-reduce(f32[1536]{0:T(1024)S(1)} %get-tuple-element.89), channel_id=1, replica_groups=mesh['seq'=128] {'seq'}, use_global_device_ids=true, to_apply=%region_3.0 | all-reduce | flops 1536 | bytes 12288 | tf_op jit(solution)/shard_map/psum | solution.py:46
  121.6 2.2 multiply_reduce_fusion.3
  123.8 64.1 %psum.36 = f32[1536]{0:T(1024)S(1)} all-reduce(f32[1536]{0:T(1024)S(1)} %multiply_reduce_fusion.3), channel_id=1, replica_groups=mesh['seq'=128] {'seq'}, use_global_device_ids=true, to_apply=%region_5.0 | all-reduce | flops 1536 | bytes 12288 | tf_op jit(solution)/shard_map/psum | solution.py:48
  188.0 9.6 %fusion.143 = (f32[1536]{0:T(1024)S(1)}, f32[1536]{0:T(1024)S(1)}, bf16[2,256,1536]{2,1,0:T(8,128)(2,1)}, f32[2,256,1536]{2,1,0:T(8,128)}) fusion(f32[1536]{0:T(1024)S(1)} %add_rsqrt_fusion, f32[2,256,1536]{2,1,0:T(8,128)} %get-tuple-element.90, f32[1536]{0:T(1024)S(1)} %broadcast_multiply_fusion, f32[1536]{0:T(1024)S(1)} %copy-done.60, ...), kind=kOutput, calls=%fused_computation.329 | convolution fusion | flops 2428498944 | bytes 14192640 | tf_op jit(solution)/shard_map/dot_general | solution.py:69
  197.6 63.0 %all-reduce.1 = (f32[1536]{0:T(1024)S(1)}, f32[1536]{0:T(1024)S(1)}) all-reduce(f32[1536]{0:T(1024)S(1)} %get-tuple-element.51, f32[1536]{0:T(1024)S(1)} %get-tuple-element.50), channel_id=1, replica_groups=mesh['seq'=128] {'seq'}, use_global_device_ids=true, to_apply=%region_9.0 | all-reduce | flops 3072 | bytes 24576 | tf_op jit(solution)/shard_map/psum | solution.py:74
  260.6 0.0 slice-start.2
  260.6 8.1 %fusion.67 = (f32[1536]{0:T(1024)S(1)}, f32[1536]{0:T(1024)S(1)}, f32[1536]{0:T(1024)S(1)}, f32[1536]{0:T(1024)S(1)}, f32[1536]{0:T(1024)S(1)}, /*index=5*/f32[1...) fusion(bf16[2,16,1536]{2,1,0:T(8,128)(2,1)S(1)} %collective-permute-done.1, ...), kind=kLoop, calls=%fused_computation.160 | loop fusion | flops 47958528 | bytes 11194368 | tf_op jit(solution)/shard_map/reduce_sum | solution.py:81
  268.8 0.0 slice-start.3
  268.8 0.0 copy-start.61
  268.8 7.1 %fusion.52 = (f32[1536]{0:T(1024)S(1)}, f32[1536]{0:T(1024)S(1)}, f32[1536]{0:T(1024)S(1)}, f32[1536]{0:T(1024)S(1)}, f32[1536]{0:T(1024)S(1)}, /*index=5*/f32[1...) fusion(f32[2,256,1536]{2,1,0:T(8,128)S(1)} %get-tuple-element.88, ...), kind=kLoop, calls=%fused_computation.145 | loop fusion | flops 40095744 | bytes 12730368 | tf_op jit(solution)/shard_map/reduce_sum | solution.py:81
  275.9 2.5 collective-permute-start.3
  278.4 3.1 collective-permute-start.2
  281.5 3.8 fusion.110
  285.3 2.8 fusion.35
  288.1 0.0 copy-start.5
  288.1 4.1 fusion.44
  292.2 5.1 %convolution_bitcast_fusion = f32[1536,1536]{0,1:T(8,128)} fusion(bf16[2,256,1536]{2,1,0:T(8,128)(2,1)S(1)} %copy-done.61, bf16[2,256,1536]{2,1,0:T(8,128)(2,1)S(1)} %copy-done.5), kind=kOutput, calls=%fused_computation.29 | convolution fusion | flops 2415919104 | bytes 12582912 | tf_op jit(solution)/shard_map/dot_general | solution.py:62
  297.7 2.8 stack.131
  300.5 0.0 all-reduce.5.cloned.1.call-update
  300.9 1.1 copy-done.4
  301.9 1.5 maximum_convert_fusion
  303.7 12.4 %fusion.68 = f32[2,256,1536]{2,1,0:T(8,128)S(1)} fusion(f32[2,288,1536]{2,1,0:T(8,128)S(1)} %maximum_convert_fusion, f32[1536]{0:T(1024)S(1)} %copy-done.48, f32[1536]{0:T(1024)S(1)} %copy-done.50, f32[1536]{0:T(1024)S(1)} %get-tuple-element.53, f32[1536]{0:T(1024)S(1)} %copy-done.8, f32[1536]{0:T(1024)S(1)} %copy-done.9, f32[1536]{0:T(1024)S(1)} %copy-done.10, ...), kind=kLoop, calls=%fused_computation.162 | loop fusion | flops 49545216 | bytes 104005632 | tf_op jit(solution)/shard_map/add | solution.py:87
  316.2 1.6 fusion.106
  317.8 9.2 %multiply_reduce_fusion.1 = (f32[512]{0:T(512)S(1)}, f32[512,1536]{1,0:T(8,128)}) fusion(f32[1536]{0:T(1024)S(1)} %copy-done.52, bf16[1536,3072]{1,0:T(8,128)(2,1)} %param.10, bf16[512,1536]{1,0:T(8,128)(2,1)S(1)} %get-tuple-element.92, bf16[512,1536]{1,0:T(8,128)(2,1)S(1)} %get-tuple-element.91), kind=kOutput, calls=%fused_computation.240 | convolution fusion | flops 4839702016 | bytes 15736832 | tf_op jit(solution)/shard_map/dot_general | solution.py:94
  327.1 2.9 multiply_reduce_fusion
  330.0 0.6 copy-done.2
  330.6 2.4 add_convert_fusion
  333.1 131.7 %all-reduce.5.cloned.1.call-done = (f32[1536,1536]{0,1:T(8,128)}, f32[32,1536]{1,0:T(8,128)}) async-done(((f32[1536,1536]{0,1:T(8,128)}, f32[32,1536]{1,0:T(8,128)}), (f32[1536,1536]{0,1:T(8,128)}, f32[32,1536]{1,0:T(8,128)})) %all-reduce.5.cloned.1.call-update) | async-done | bytes 9633808
  464.7 1.7 constant_dynamic-slice_fusion
  466.4 0.9 copy.17
  467.3 1.6 copy.23
  (168 shorter events, 0.5 us)
Async XLA Ops:
  7.2 3.9 copy-start.1
  7.2 3.9 copy-start.51
  7.2 457.6 %all-reduce.5.cloned.1.call-start = ((), (), s32[]{:S(2)}) async-start(), calls=%async_computation | async-start | bytes 19267584
  19.2 10.1 %copy-start.7 = (f32[32,1536]{1,0:T(8,128)S(1)}, f32[32,1536]{1,0:T(8,128)}, u32[]{:S(2)}) copy-start(f32[32,1536]{1,0:T(8,128)} %param.11) | copy-start | bytes 589828
  22.5 8.1 %collective-permute-start.1 = (bf16[2,16,1536]{2,1,0:T(8,128)(2,1)}, bf16[2,16,1536]{2,1,0:T(8,128)(2,1)S(1)}, u32[]{:S(2)}, u32[]{:S(2)}) collective-permute-start(bf16[2,16,1536]{2,1,0:T(8,128)(2,1)} %get-tuple-element.98), channel_id=1, source_target_pairs={{1,0},{2,1},{3,2},{4,3},{5,4},{6,5},{7,6},{8,7},{9,8},{10,9},{11,1... | collective-permute-start | bytes 294920 | tf_op jit(solution)/shard_map/ppermute | solution.py:21
  25.8 5.5 %collective-permute-start = (bf16[2,16,1536]{2,1,0:T(8,128)(2,1)}, bf16[2,16,1536]{2,1,0:T(8,128)(2,1)S(1)}, u32[]{:S(2)}, u32[]{:S(2)}) collective-permute-start(bf16[2,16,1536]{2,1,0:T(8,128)(2,1)} %get-tuple-element.97), channel_id=1, source_target_pairs={{0,1},{1,2},{2,3},{3,4},{4,5},{5,6},{6,7},{7,8},{8,9},{9,10},{10,1... | collective-permute-start | bytes 294920 | tf_op jit(solution)/shard_map/ppermute | solution.py:18
  30.5 17.9 %copy-start.27 = (f32[1536]{0:T(1024)}, f32[1536]{0:T(1024)S(1)}, u32[]{:S(2)}) copy-start(f32[1536]{0:T(1024)S(1)} %get-tuple-element.72) | copy-start | bytes 18436
  30.5 17.9 %copy-start.29 = (f32[1536]{0:T(1024)}, f32[1536]{0:T(1024)S(1)}, u32[]{:S(2)}) copy-start(f32[1536]{0:T(1024)S(1)} %get-tuple-element.73) | copy-start | bytes 18436
  30.5 17.9 %copy-start.31 = (f32[1536]{0:T(1024)}, f32[1536]{0:T(1024)S(1)}, u32[]{:S(2)}) copy-start(f32[1536]{0:T(1024)S(1)} %get-tuple-element.74) | copy-start | bytes 18436
  30.5 17.9 %copy-start.33 = (f32[1536]{0:T(1024)}, f32[1536]{0:T(1024)S(1)}, u32[]{:S(2)}) copy-start(f32[1536]{0:T(1024)S(1)} %get-tuple-element.75) | copy-start | bytes 18436
  30.5 17.9 %copy-start.35 = (f32[1536]{0:T(1024)}, f32[1536]{0:T(1024)S(1)}, u32[]{:S(2)}) copy-start(f32[1536]{0:T(1024)S(1)} %get-tuple-element.76) | copy-start | bytes 18436
  30.5 17.9 %copy-start.37 = (f32[1536]{0:T(1024)}, f32[1536]{0:T(1024)S(1)}, u32[]{:S(2)}) copy-start(f32[1536]{0:T(1024)S(1)} %get-tuple-element.77) | copy-start | bytes 18436
  30.5 17.9 %copy-start.39 = (f32[1536]{0:T(1024)}, f32[1536]{0:T(1024)S(1)}, u32[]{:S(2)}) copy-start(f32[1536]{0:T(1024)S(1)} %get-tuple-element.78) | copy-start | bytes 18436
  30.6 17.9 %copy-start.41 = (f32[1536]{0:T(1024)}, f32[1536]{0:T(1024)S(1)}, u32[]{:S(2)}) copy-start(f32[1536]{0:T(1024)S(1)} %get-tuple-element.79) | copy-start | bytes 18436
  30.6 17.9 %copy-start.43 = (f32[1536]{0:T(1024)}, f32[1536]{0:T(1024)S(1)}, u32[]{:S(2)}) copy-start(f32[1536]{0:T(1024)S(1)} %get-tuple-element.80) | copy-start | bytes 18436
  30.6 17.9 %copy-start.45 = (f32[1536]{0:T(1024)}, f32[1536]{0:T(1024)S(1)}, u32[]{:S(2)}) copy-start(f32[1536]{0:T(1024)S(1)} %get-tuple-element.81) | copy-start | bytes 18436
  30.6 17.9 %copy-start.47 = (f32[1536]{0:T(1024)}, f32[1536]{0:T(1024)S(1)}, u32[]{:S(2)}) copy-start(f32[1536]{0:T(1024)S(1)} %get-tuple-element.82) | copy-start | bytes 18436
  30.6 17.9 %copy-start.49 = (f32[1536]{0:T(1024)}, f32[1536]{0:T(1024)S(1)}, u32[]{:S(2)}) copy-start(f32[1536]{0:T(1024)S(1)} %get-tuple-element.83) | copy-start | bytes 18436
  31.3 156.7 %copy-start.57 = (f32[1536]{0:T(1024)S(1)}, f32[1536]{0:T(1024)}, u32[]{:S(2)}) copy-start(f32[1536]{0:T(1024)} %param.12) | copy-start | bytes 18436
  31.3 156.7 %copy-start.60 = (f32[1536]{0:T(1024)S(1)}, f32[1536]{0:T(1024)}, u32[]{:S(2)}) copy-start(f32[1536]{0:T(1024)} %param.13) | copy-start | bytes 18436
  260.6 8.2 %copy-start.58 = (f32[1536]{0:T(1024)}, f32[1536]{0:T(1024)S(1)}, u32[]{:S(2)}) copy-start(f32[1536]{0:T(1024)S(1)} %get-tuple-element.108) | copy-start | bytes 18436
  260.6 8.2 %copy-start.59 = (f32[1536]{0:T(1024)}, f32[1536]{0:T(1024)S(1)}, u32[]{:S(2)}) copy-start(f32[1536]{0:T(1024)S(1)} %get-tuple-element.109) | copy-start | bytes 18436
  260.6 20.9 %slice-start.2 = ((s8[4718592]{0:T(1024)(128)(4,1)}), s8[4194304]{0:T(1024)(128)(4,1)S(1)}, s32[]{:S(2)}) async-start(s8[4718592]{0:T(1024)(128)(4,1)} %bitcast.52), calls=%async_computation.3 | async-start | bytes 8388608
  268.8 12.7 %slice-start.3 = ((s8[4718592]{0:T(1024)(128)(4,1)}), s8[524288]{0:T(1024)(128)(4,1)S(1)}, s32[]{:S(2)}) async-start(s8[4718592]{0:T(1024)(128)(4,1)} %bitcast.52), calls=%async_computation.4 | async-start | bytes 1048576
  268.8 12.7 %copy-start.61 = (bf16[2,256,1536]{2,1,0:T(8,128)(2,1)S(1)}, bf16[2,256,1536]{2,1,0:T(8,128)(2,1)}, u32[]{:S(2)}) copy-start(bf16[2,256,1536]{2,1,0:T(8,128)(2,1)} %get-tuple-element.93) | copy-start | bytes 4718596
  275.9 9.4 %copy-start.3 = (bf16[2,256,1536]{2,1,0:T(8,128)(2,1)}, bf16[2,256,1536]{2,1,0:T(8,128)(2,1)S(1)}, u32[]{:S(2)}) copy-start(bf16[2,256,1536]{2,1,0:T(8,128)(2,1)S(1)} %get-tuple-element.94) | copy-start | bytes 4718596
  275.9 24.9 %collective-permute-start.3 = (bf16[2,16,1536]{2,1,0:T(8,128)(2,1)S(1)}, bf16[2,16,1536]{2,1,0:T(8,128)(2,1)S(1)}, u32[]{:S(2)}, u32[]{:S(2)}) collective-permute-start(bf16[2,16,1536]{2,1,0:T(8,128)(2,1)S(1)} %get-tuple-element.96), channel_id=1, source_target_pairs={{1,0},{2,1},{3,2},{4,3},{5,4},{6,5},{7,6},{8,7},{9,8},{10,9},{11,1... | collective-permute-start | bytes 294920 | tf_op jit(solution)/shard_map/ppermute | solution.py:21
  278.4 22.4 %collective-permute-start.2 = (bf16[2,16,1536]{2,1,0:T(8,128)(2,1)S(1)}, bf16[2,16,1536]{2,1,0:T(8,128)(2,1)}, u32[]{:S(2)}, u32[]{:S(2)}) collective-permute-start(bf16[2,16,1536]{2,1,0:T(8,128)(2,1)S(1)} %get-tuple-element.95), channel_id=1, source_target_pairs={{0,1},{1,2},{2,3},{3,4},{4,5},{5,6},{6,7},{7,8},{8,9},{9,10},{10,1... | collective-permute-start | bytes 294920 | tf_op jit(solution)/shard_map/ppermute | solution.py:18
  288.1 4.1 copy-start.5
  300.5 2.9 copy-start.8
  300.5 2.9 copy-start.9
  300.5 2.9 copy-start.10
  300.6 2.9 copy-start.11
  300.6 2.9 copy-start.12
  300.6 2.9 copy-start.13
  300.6 2.9 copy-start.14
  300.6 2.9 copy-start.15
  300.6 2.9 copy-start.16
  300.6 2.9 copy-start.17
  300.6 2.9 copy-start.18
  300.6 2.9 copy-start.19
  300.6 2.9 copy-start.20
  301.9 14.2 %slice-start = ((s8[6291456]{0:T(1024)(128)(4,1)}), s8[4194304]{0:T(1024)(128)(4,1)S(1)}, s32[]{:S(2)}) async-start(s8[6291456]{0:T(1024)(128)(4,1)} %bitcast.47), calls=%async_computation.1 | async-start | bytes 8388608
  303.7 12.4 %slice-start.1 = ((s8[6291456]{0:T(1024)(128)(4,1)}), s8[2097152]{0:T(1024)(128)(4,1)S(1)}, s32[]{:S(2)}) async-start(s8[6291456]{0:T(1024)(128)(4,1)} %bitcast.47), calls=%async_computation.2 | async-start | bytes 4194304
  317.8 9.3 %copy-start.54 = (f32[2,256]{1,0:T(2,128)S(1)}, f32[2,256]{1,0:T(2,128)}, u32[]{:S(2)}) copy-start(f32[2,256]{1,0:T(2,128)} %copy-done.53) | copy-start | bytes 6148
  317.8 9.3 %copy-start.56 = (f32[2,256]{1,0:T(2,128)S(1)}, f32[2,256]{1,0:T(2,128)}, u32[]{:S(2)}) copy-start(f32[2,256]{1,0:T(2,128)} %copy-done.55) | copy-start | bytes 6148
  327.0 3.0 copy-start.6
  327.0 3.6 copy-start.2
  (23 other events, 58.8 us)
Sparse Core Ops, SparseCore 0:
  300.6 164.0 all-reduce.4
where the time goes:
time: 477 us; the launch traced here: 476 us
  blocking collectives  200 us (42%)
  waiting for transfers between devices  132 us (28%)
  other arithmetic  67.4 us (14%)
  matrix products  35.3 us (7%)
  between operations  15.4 us (3%)
  local copies, waits for them, and re-layouts  12.7 us (3%)
  starting transfers between devices  12.4 us (3%)
    unnamed x2, waiting for transfers between devices  132 us
    psum x1, blocking collectives, on_device(): bn_mean = lax.psum(jnp.sum(conv_out, axis=(0, 1)), 'seq') / frame_total  73.1 us
    psum x1, blocking collectives, on_device(): lax.psum(jnp.sum(deviate * deviate, axis=(0, 1)), 'seq') / frame_total  64.1 us
    psum x1, blocking collectives, on_device(): d_bn_bias, d_bn_gain = lax.psum((local_bias, local_gain), 'seq')  63 us
    reduce_sum x4, other arithmetic, on_device(): kernel_rows.append(jnp.sum(window * d_conv, axis=(0, 1)))  22 us
    reduce_sum x1, other arithmetic, on_device(): bn_mean = lax.psum(jnp.sum(conv_out, axis=(0, 1)), 'seq') / frame_total  17.2 us
    add x1, other arithmetic, on_device(): d_gated + kernel[tap_index] * grad_padded[:, 31 - tap_index:31 - tap_inde...  12.4 us
    dot_general x1, matrix products, on_device(): d_act = jnp.dot(cot_rows, w_out, preferred_element_type=jnp.float32)  9.63 us
  transfers between devices with their start and end apart: 5, of which 2 were waited for; matrix products, arithmetic and copies ran while one was open for 10% of the time, Pallas kernels for 0%

commit v1 on v0

--- a/solution.py
+++ b/solution.py
@@ -24,6 +24,11 @@
 
 
 def on_device(inputs, ln_gain, w_in, kernel, bn_gain, bn_bias, w_out, cotangent):
+
+    def _plan_target(piece_in):
+        work_now = lax.all_gather(piece_in, axis_name="seq")
+        return jnp.sum(work_now, axis=0)
+
     devices_seq = lax.axis_size("seq")
     frame_total = UTT * FRAMES_DEV * devices_seq
     rows_here = UTT * FRAMES_DEV
@@ -43,7 +48,7 @@
         conv_out = conv_out + kernel[tap_index] * padded[
             :, tap_index + 1 : tap_index + 1 + FRAMES_DEV
         ].astype(jnp.float32)
-    bn_mean = lax.psum(jnp.sum(conv_out, axis=(0, 1)), "seq") / frame_total
+    bn_mean = _plan_target(jnp.sum(conv_out, axis=(0, 1))) / frame_total
     deviate = conv_out - bn_mean
     bn_var = lax.psum(jnp.sum(deviate * deviate, axis=(0, 1)), "seq") / frame_total
     bn_rstd = lax.rsqrt(bn_var + EPSILON)

time: 477 us -> 454 us (0.952)
  blocking collectives: 200 us -> 175 us
    psum x1 -> x0, blocking collectives: 73.1 us -> none  [on_device(): bn_mean = lax.psum(jnp.sum(conv_out, axis=(0, 1)), 'seq') / frame_total]
    all_gather x0 -> x1, blocking collectives: none -> 48.3 us  [_plan_target(): work_now = lax.all_gather(piece_in, axis_name='seq')]
    reduce_sum x1 -> x2, other arithmetic: 17.2 us -> 18.8 us  [the longest x1 17.2 us: on_device(): bn_mean = _plan_target(jnp.sum(conv_out, axis=(0, 1))) / frame_total]
  transfers between devices with their start and end apart: 5 -> 5, of which waited for: 2 -> 2; matrix products, arithmetic and copies ran while one was open for 10% -> 11% of each run, Pallas kernels for 0% -> 0%
where the time goes in v1:
time: 454 us; the launch traced here: 453 us
  blocking collectives  175 us (39%)
  waiting for transfers between devices  132 us (29%)
  other arithmetic  69.1 us (15%)
  matrix products  35.3 us (8%)
  between operations  15.4 us (3%)
  local copies, waits for them, and re-layouts  12.8 us (3%)
  starting transfers between devices  12.7 us (3%)
    unnamed x2, waiting for transfers between devices  132 us
    psum x1, blocking collectives, on_device(): lax.psum(jnp.sum(deviate * deviate, axis=(0, 1)), 'seq') / frame_total  64.3 us
    psum x1, blocking collectives, on_device(): d_bn_bias, d_bn_gain = lax.psum((local_bias, local_gain), 'seq')  62.8 us
    all_gather x1, blocking collectives, _plan_target(): work_now = lax.all_gather(piece_in, axis_name='seq')  48.3 us
    reduce_sum x4, other arithmetic, on_device(): kernel_rows.append(jnp.sum(window * d_conv, axis=(0, 1)))  22 us
    reduce_sum x1, other arithmetic, on_device(): bn_mean = _plan_target(jnp.sum(conv_out, axis=(0, 1))) / frame_total  17.2 us
    add x1, other arithmetic, on_device(): d_gated + kernel[tap_index] * grad_padded[:, 31 - tap_index:31 - tap_inde...  12.4 us
    dot_general x1, matrix products, on_device(): d_act = jnp.dot(cot_rows, w_out, preferred_element_type=jnp.float32)  9.63 us
  transfers between devices with their start and end apart: 5, of which 2 were waited for; matrix products, arithmetic and copies ran while one was open for 11% of the time, Pallas kernels for 0%

profile of v1, /device:TPU:1, one launch (start us, length us, event | category | flops | bytes accessed | tf_op | source)
XLA Modules:
  0.0 452.8 jit_solution(14320021581299311621)
XLA Ops:
  7.2 0.0 copy-start.51
  7.2 0.0 all-reduce.5.cloned.1.call-start
  7.2 1.8 convert_reduce_fusion
  9.1 2.0 multiply_reduce_fusion.4
  11.0 0.5 multiply_convert_fusion.1
  11.6 0.0 copy-done.55
  11.6 7.6 %fusion.148 = f32[512,3072]{1,0:T(8,128)S(1)} fusion(bf16[512,1536]{1,0:T(8,128)(2,1)S(1)} %bitcast.51, bf16[1536,3072]{1,0:T(8,128)(2,1)} %param.10), kind=kOutput, calls=%fused_computation.333 | convolution fusion | flops 4831838208 | bytes 17301504 | tf_op jit(solution)/shard_map/dot_general | solution.py:41
  19.2 0.8 multiply_convert_fusion
  20.1 1.7 copy-done
  21.8 0.7 fusion.147
  22.5 3.3 collective-permute-start.1
  25.8 3.6 collective-permute-start
  29.3 0.9 slice_reduce_fusion.31
  30.3 0.2 slice_reduce_fusion.30
  30.6 0.7 collective-permute-done
  31.3 17.2 %fusion.144 = (f32[1536]{0:T(1024)S(1)}, f32[2,256,1536]{2,1,0:T(8,128)}) fusion(bf16[2,16,1536]{2,1,0:T(8,128)(2,1)S(1)} %collective-permute-done.1, bf16[2,256,1536]{2,1,0:T(8,128)(2,1)S(1)} %bitcast.42, f32[1536]{0:T(1024)S(1)} %get-tuple-element.82, f32[1536]{0:T(1024)S(1)} %get-tuple-element.83, f32[1536]{0:T(1024)S(1)} %get-tuple-element.53, ...), kind=kLoop, calls=%fused_computation.330 | loop fusion | flops 148634112 | bytes 5117952 | tf_op jit(solution)/shard_map/reduce_sum | solution.py:51
  48.4 0.0 copy-start.60
  48.6 48.3 %all-gather.1 = f32[128,1,1536]{2,1,0:T(1,128)} all-gather(f32[1,1,1536]{2,1,0:T(1,128)S(1)} %reshape.112), channel_id=2, replica_groups=mesh['seq'=128] {'seq'}, dimensions={0}, use_global_device_ids=true | all-gather | bytes 792576 | tf_op jit(solution)/shard_map/all_gather | solution.py:29
  96.9 1.6 reduce_sum.372
  98.5 2.2 multiply_reduce_fusion.3
  100.7 64.3 %psum.28 = f32[1536]{0:T(1024)S(1)} all-reduce(f32[1536]{0:T(1024)S(1)} %multiply_reduce_fusion.3), channel_id=1, replica_groups=mesh['seq'=128] {'seq'}, use_global_device_ids=true, to_apply=%region_5.0 | all-reduce | flops 1536 | bytes 12288 | tf_op jit(solution)/shard_map/psum | solution.py:53
  165.0 9.6 %fusion.143 = (f32[1536]{0:T(1024)S(1)}, f32[1536]{0:T(1024)S(1)}, bf16[2,256,1536]{2,1,0:T(8,128)(2,1)}, f32[2,256,1536]{2,1,0:T(8,128)}) fusion(f32[1536]{0:T(1024)S(1)} %add_rsqrt_fusion, f32[2,256,1536]{2,1,0:T(8,128)} %get-tuple-element.90, f32[1536]{0:T(1024)S(1)} %broadcast_multiply_fusion, f32[1536]{0:T(1024)S(1)} %copy-done.60, ...), kind=kOutput, calls=%fused_computation.329 | convolution fusion | flops 2428498944 | bytes 14192640 | tf_op jit(solution)/shard_map/dot_general | solution.py:74
  174.7 62.8 %all-reduce.1 = (f32[1536]{0:T(1024)S(1)}, f32[1536]{0:T(1024)S(1)}) all-reduce(f32[1536]{0:T(1024)S(1)} %get-tuple-element.51, f32[1536]{0:T(1024)S(1)} %get-tuple-element.50), channel_id=1, replica_groups=mesh['seq'=128] {'seq'}, use_global_device_ids=true, to_apply=%region_9.0 | all-reduce | flops 3072 | bytes 24576 | tf_op jit(solution)/shard_map/psum | solution.py:79
  237.5 0.0 slice-start.2
  237.5 8.1 %fusion.67 = (f32[1536]{0:T(1024)S(1)}, f32[1536]{0:T(1024)S(1)}, f32[1536]{0:T(1024)S(1)}, f32[1536]{0:T(1024)S(1)}, f32[1536]{0:T(1024)S(1)}, /*index=5*/f32[1...) fusion(bf16[2,16,1536]{2,1,0:T(8,128)(2,1)S(1)} %collective-permute-done.1, ...), kind=kLoop, calls=%fused_computation.160 | loop fusion | flops 47958528 | bytes 11194368 | tf_op jit(solution)/shard_map/reduce_sum | solution.py:86
  245.6 0.0 slice-start.3
  245.6 0.0 copy-start.61
  245.7 7.1 %fusion.52 = (f32[1536]{0:T(1024)S(1)}, f32[1536]{0:T(1024)S(1)}, f32[1536]{0:T(1024)S(1)}, f32[1536]{0:T(1024)S(1)}, f32[1536]{0:T(1024)S(1)}, /*index=5*/f32[1...) fusion(f32[2,256,1536]{2,1,0:T(8,128)S(1)} %get-tuple-element.88, ...), kind=kLoop, calls=%fused_computation.145 | loop fusion | flops 40095744 | bytes 12730368 | tf_op jit(solution)/shard_map/reduce_sum | solution.py:86
  252.8 2.5 collective-permute-start.3
  255.2 3.3 collective-permute-start.2
  258.6 3.8 fusion.110
  262.4 2.8 fusion.35
  265.2 4.1 fusion.44
  269.3 5.1 %convolution_bitcast_fusion = f32[1536,1536]{0,1:T(8,128)} fusion(bf16[2,256,1536]{2,1,0:T(8,128)(2,1)S(1)} %copy-done.61, bf16[2,256,1536]{2,1,0:T(8,128)(2,1)S(1)} %copy-done.5), kind=kOutput, calls=%fused_computation.29 | convolution fusion | flops 2415919104 | bytes 12582912 | tf_op jit(solution)/shard_map/dot_general | solution.py:67
  274.8 2.8 stack.131
  277.6 0.0 all-reduce.5.cloned.1.call-update
  277.9 1.1 copy-done.4
  279.0 1.5 maximum_convert_fusion
  280.8 12.4 %fusion.68 = f32[2,256,1536]{2,1,0:T(8,128)S(1)} fusion(f32[2,288,1536]{2,1,0:T(8,128)S(1)} %maximum_convert_fusion, f32[1536]{0:T(1024)S(1)} %copy-done.48, f32[1536]{0:T(1024)S(1)} %copy-done.50, f32[1536]{0:T(1024)S(1)} %get-tuple-element.53, f32[1536]{0:T(1024)S(1)} %copy-done.8, f32[1536]{0:T(1024)S(1)} %copy-done.9, f32[1536]{0:T(1024)S(1)} %copy-done.10, ...), kind=kLoop, calls=%fused_computation.162 | loop fusion | flops 49545216 | bytes 104005632 | tf_op jit(solution)/shard_map/add | solution.py:92
  293.3 1.6 fusion.106
  294.9 9.2 %multiply_reduce_fusion.1 = (f32[512]{0:T(512)S(1)}, f32[512,1536]{1,0:T(8,128)}) fusion(f32[1536]{0:T(1024)S(1)} %copy-done.52, bf16[1536,3072]{1,0:T(8,128)(2,1)} %param.10, bf16[512,1536]{1,0:T(8,128)(2,1)S(1)} %get-tuple-element.92, bf16[512,1536]{1,0:T(8,128)(2,1)S(1)} %get-tuple-element.91), kind=kOutput, calls=%fused_computation.240 | convolution fusion | flops 4839702016 | bytes 15736832 | tf_op jit(solution)/shard_map/dot_general | solution.py:99
  304.1 3.0 multiply_reduce_fusion
  307.1 0.6 copy-done.2
  307.8 2.4 add_convert_fusion
  310.2 131.6 %all-reduce.5.cloned.1.call-done = (f32[1536,1536]{0,1:T(8,128)}, f32[32,1536]{1,0:T(8,128)}) async-done(((f32[1536,1536]{0,1:T(8,128)}, f32[32,1536]{1,0:T(8,128)}), (f32[1536,1536]{0,1:T(8,128)}, f32[32,1536]{1,0:T(8,128)})) %all-reduce.5.cloned.1.call-update) | async-done | bytes 9633808
  441.8 1.7 constant_dynamic-slice_fusion
  443.4 0.9 copy.17
  444.4 1.6 copy.23
  (170 shorter events, 0.6 us)
Async XLA Ops:
  7.2 3.9 copy-start.1
  7.2 3.9 copy-start.51
  7.2 434.6 %all-reduce.5.cloned.1.call-start = ((), (), s32[]{:S(2)}) async-start(), calls=%async_computation | async-start | bytes 19267584
  19.2 10.1 %copy-start.7 = (f32[32,1536]{1,0:T(8,128)S(1)}, f32[32,1536]{1,0:T(8,128)}, u32[]{:S(2)}) copy-start(f32[32,1536]{1,0:T(8,128)} %param.11) | copy-start | bytes 589828
  22.5 8.1 %collective-permute-start.1 = (bf16[2,16,1536]{2,1,0:T(8,128)(2,1)}, bf16[2,16,1536]{2,1,0:T(8,128)(2,1)S(1)}, u32[]{:S(2)}, u32[]{:S(2)}) collective-permute-start(bf16[2,16,1536]{2,1,0:T(8,128)(2,1)} %get-tuple-element.98), channel_id=1, source_target_pairs={{1,0},{2,1},{3,2},{4,3},{5,4},{6,5},{7,6},{8,7},{9,8},{10,9},{11,1... | collective-permute-start | bytes 294920 | tf_op jit(solution)/shard_map/ppermute | solution.py:21
  25.8 5.5 %collective-permute-start = (bf16[2,16,1536]{2,1,0:T(8,128)(2,1)}, bf16[2,16,1536]{2,1,0:T(8,128)(2,1)S(1)}, u32[]{:S(2)}, u32[]{:S(2)}) collective-permute-start(bf16[2,16,1536]{2,1,0:T(8,128)(2,1)} %get-tuple-element.97), channel_id=1, source_target_pairs={{0,1},{1,2},{2,3},{3,4},{4,5},{5,6},{6,7},{7,8},{8,9},{9,10},{10,1... | collective-permute-start | bytes 294920 | tf_op jit(solution)/shard_map/ppermute | solution.py:18
  30.5 17.9 %copy-start.27 = (f32[1536]{0:T(1024)}, f32[1536]{0:T(1024)S(1)}, u32[]{:S(2)}) copy-start(f32[1536]{0:T(1024)S(1)} %get-tuple-element.72) | copy-start | bytes 18436
  30.5 18.0 %copy-start.29 = (f32[1536]{0:T(1024)}, f32[1536]{0:T(1024)S(1)}, u32[]{:S(2)}) copy-start(f32[1536]{0:T(1024)S(1)} %get-tuple-element.73) | copy-start | bytes 18436
  30.5 18.0 %copy-start.31 = (f32[1536]{0:T(1024)}, f32[1536]{0:T(1024)S(1)}, u32[]{:S(2)}) copy-start(f32[1536]{0:T(1024)S(1)} %get-tuple-element.74) | copy-start | bytes 18436
  30.5 18.0 %copy-start.33 = (f32[1536]{0:T(1024)}, f32[1536]{0:T(1024)S(1)}, u32[]{:S(2)}) copy-start(f32[1536]{0:T(1024)S(1)} %get-tuple-element.75) | copy-start | bytes 18436
  30.5 18.0 %copy-start.35 = (f32[1536]{0:T(1024)}, f32[1536]{0:T(1024)S(1)}, u32[]{:S(2)}) copy-start(f32[1536]{0:T(1024)S(1)} %get-tuple-element.76) | copy-start | bytes 18436
  30.5 18.0 %copy-start.37 = (f32[1536]{0:T(1024)}, f32[1536]{0:T(1024)S(1)}, u32[]{:S(2)}) copy-start(f32[1536]{0:T(1024)S(1)} %get-tuple-element.77) | copy-start | bytes 18436
  30.5 18.0 %copy-start.39 = (f32[1536]{0:T(1024)}, f32[1536]{0:T(1024)S(1)}, u32[]{:S(2)}) copy-start(f32[1536]{0:T(1024)S(1)} %get-tuple-element.78) | copy-start | bytes 18436
  30.6 18.0 %copy-start.41 = (f32[1536]{0:T(1024)}, f32[1536]{0:T(1024)S(1)}, u32[]{:S(2)}) copy-start(f32[1536]{0:T(1024)S(1)} %get-tuple-element.79) | copy-start | bytes 18436
  30.6 18.0 %copy-start.43 = (f32[1536]{0:T(1024)}, f32[1536]{0:T(1024)S(1)}, u32[]{:S(2)}) copy-start(f32[1536]{0:T(1024)S(1)} %get-tuple-element.80) | copy-start | bytes 18436
  30.6 18.0 %copy-start.45 = (f32[1536]{0:T(1024)}, f32[1536]{0:T(1024)S(1)}, u32[]{:S(2)}) copy-start(f32[1536]{0:T(1024)S(1)} %get-tuple-element.81) | copy-start | bytes 18436
  30.6 18.0 %copy-start.47 = (f32[1536]{0:T(1024)}, f32[1536]{0:T(1024)S(1)}, u32[]{:S(2)}) copy-start(f32[1536]{0:T(1024)S(1)} %get-tuple-element.82) | copy-start | bytes 18436
  30.6 18.0 %copy-start.49 = (f32[1536]{0:T(1024)}, f32[1536]{0:T(1024)S(1)}, u32[]{:S(2)}) copy-start(f32[1536]{0:T(1024)S(1)} %get-tuple-element.83) | copy-start | bytes 18436
  48.4 116.6 %copy-start.57 = (f32[1536]{0:T(1024)S(1)}, f32[1536]{0:T(1024)}, u32[]{:S(2)}) copy-start(f32[1536]{0:T(1024)} %param.12) | copy-start | bytes 18436
  48.4 116.6 %copy-start.60 = (f32[1536]{0:T(1024)S(1)}, f32[1536]{0:T(1024)}, u32[]{:S(2)}) copy-start(f32[1536]{0:T(1024)} %param.13) | copy-start | bytes 18436
  237.4 8.2 %copy-start.58 = (f32[1536]{0:T(1024)}, f32[1536]{0:T(1024)S(1)}, u32[]{:S(2)}) copy-start(f32[1536]{0:T(1024)S(1)} %get-tuple-element.108) | copy-start | bytes 18436
  237.5 8.2 %copy-start.59 = (f32[1536]{0:T(1024)}, f32[1536]{0:T(1024)S(1)}, u32[]{:S(2)}) copy-start(f32[1536]{0:T(1024)S(1)} %get-tuple-element.109) | copy-start | bytes 18436
  237.5 21.1 %slice-start.2 = ((s8[4718592]{0:T(1024)(128)(4,1)}), s8[4194304]{0:T(1024)(128)(4,1)S(1)}, s32[]{:S(2)}) async-start(s8[4718592]{0:T(1024)(128)(4,1)} %bitcast.52), calls=%async_computation.3 | async-start | bytes 8388608
  245.6 12.9 %slice-start.3 = ((s8[4718592]{0:T(1024)(128)(4,1)}), s8[524288]{0:T(1024)(128)(4,1)S(1)}, s32[]{:S(2)}) async-start(s8[4718592]{0:T(1024)(128)(4,1)} %bitcast.52), calls=%async_computation.4 | async-start | bytes 1048576
  245.6 12.9 %copy-start.61 = (bf16[2,256,1536]{2,1,0:T(8,128)(2,1)S(1)}, bf16[2,256,1536]{2,1,0:T(8,128)(2,1)}, u32[]{:S(2)}) copy-start(bf16[2,256,1536]{2,1,0:T(8,128)(2,1)} %get-tuple-element.93) | copy-start | bytes 4718596
  252.7 9.6 %copy-start.3 = (bf16[2,256,1536]{2,1,0:T(8,128)(2,1)}, bf16[2,256,1536]{2,1,0:T(8,128)(2,1)S(1)}, u32[]{:S(2)}) copy-start(bf16[2,256,1536]{2,1,0:T(8,128)(2,1)S(1)} %get-tuple-element.94) | copy-start | bytes 4718596
  252.8 25.2 %collective-permute-start.3 = (bf16[2,16,1536]{2,1,0:T(8,128)(2,1)S(1)}, bf16[2,16,1536]{2,1,0:T(8,128)(2,1)S(1)}, u32[]{:S(2)}, u32[]{:S(2)}) collective-permute-start(bf16[2,16,1536]{2,1,0:T(8,128)(2,1)S(1)} %get-tuple-element.96), channel_id=1, source_target_pairs={{1,0},{2,1},{3,2},{4,3},{5,4},{6,5},{7,6},{8,7},{9,8},{10,9},{11,1... | collective-permute-start | bytes 294920 | tf_op jit(solution)/shard_map/ppermute | solution.py:21
  255.2 22.7 %collective-permute-start.2 = (bf16[2,16,1536]{2,1,0:T(8,128)(2,1)S(1)}, bf16[2,16,1536]{2,1,0:T(8,128)(2,1)}, u32[]{:S(2)}, u32[]{:S(2)}) collective-permute-start(bf16[2,16,1536]{2,1,0:T(8,128)(2,1)S(1)} %get-tuple-element.95), channel_id=1, source_target_pairs={{0,1},{1,2},{2,3},{3,4},{4,5},{5,6},{6,7},{7,8},{8,9},{9,10},{10,1... | collective-permute-start | bytes 294920 | tf_op jit(solution)/shard_map/ppermute | solution.py:18
  265.1 4.1 copy-start.5
  277.6 2.9 copy-start.8
  277.6 2.9 copy-start.9
  277.6 2.9 copy-start.10
  277.6 2.9 copy-start.11
  277.6 2.9 copy-start.12
  277.7 2.9 copy-start.13
  277.7 2.9 copy-start.14
  277.7 2.9 copy-start.15
  277.7 2.9 copy-start.16
  277.7 2.9 copy-start.17
  277.7 2.9 copy-start.18
  277.7 2.9 copy-start.19
  277.7 2.9 copy-start.20
  279.0 14.2 %slice-start = ((s8[6291456]{0:T(1024)(128)(4,1)}), s8[4194304]{0:T(1024)(128)(4,1)S(1)}, s32[]{:S(2)}) async-start(s8[6291456]{0:T(1024)(128)(4,1)} %bitcast.47), calls=%async_computation.1 | async-start | bytes 8388608
  280.8 12.4 %slice-start.1 = ((s8[6291456]{0:T(1024)(128)(4,1)}), s8[2097152]{0:T(1024)(128)(4,1)S(1)}, s32[]{:S(2)}) async-start(s8[6291456]{0:T(1024)(128)(4,1)} %bitcast.47), calls=%async_computation.2 | async-start | bytes 4194304
  294.8 9.3 %copy-start.54 = (f32[2,256]{1,0:T(2,128)S(1)}, f32[2,256]{1,0:T(2,128)}, u32[]{:S(2)}) copy-start(f32[2,256]{1,0:T(2,128)} %copy-done.53) | copy-start | bytes 6148
  294.8 9.3 %copy-start.56 = (f32[2,256]{1,0:T(2,128)S(1)}, f32[2,256]{1,0:T(2,128)}, u32[]{:S(2)}) copy-start(f32[2,256]{1,0:T(2,128)} %copy-done.55) | copy-start | bytes 6148
  304.1 3.0 copy-start.6
  304.1 3.6 copy-start.2
  (23 other events, 58.8 us)
Sparse Core Ops, SparseCore 0:
  277.7 164.0 all-reduce.4
